TPU v7x, 32 devices: a whole 2x2x4 slice. The times are simulated.
32 devices in a mesh: wide: 8 (over z, x), narrow: 4 (over y, core).
Axes of the slice: x: 2, y: 2, z: 4, core: 2. Of those that a mesh axis runs over, the one named last changes fastest.
Arguments:
- moments: float32 [4096, 2048], P('wide', 'narrow'), as said below
- eigen_basis: float32 [4096, 2048], P('wide', 'narrow'), may hold values from -0.125 to 0.125
- slot_order: int32 [2], replicated, may hold values 0 or 1
Outputs:
- halves: float32 [4096, 1024], P('wide', 'narrow')
Inputs may be any that keep to these rules, and one draw needn't show every extreme that they name: Each block of 2048 rows of moments is symmetric.
All inputs are finite; a program needn't handle non-finite values.
Results may differ from a plain program's by a relative error of at most 0.0001.
Values sent between devices are 32-bit elements; how exact they have to be, the bound alone decides.
A program may use at most 64 MiB of HBM per device.

v0:
```python
import jax
import jax.numpy as jnp
from jax import lax
from jax.sharding import PartitionSpec as P

GROUP_WIDE = 4
K = 1024


def partner(value, axis, stride):
    mask = 2**stride
    pairs = [(source, source ^ mask) for source in range(lax.axis_size(axis))]
    return lax.ppermute(value, axis, pairs)


def body(moments, eigen_basis, slot_order):
    wide_pos = lax.axis_index("wide")
    subproblem = wide_pos // GROUP_WIDE
    position = wide_pos % GROUP_WIDE
    swapped = lax.dynamic_index_in_dim(slot_order, subproblem, 0, keepdims=False)
    narrow_pos = lax.axis_index("narrow")
    col_count = eigen_basis.shape[1]
    half_cols = col_count // 2
    full_basis = lax.all_gather(eigen_basis, "narrow", axis=1, tiled=True)
    first_half = lax.dynamic_slice_in_dim(full_basis, narrow_pos * half_cols, half_cols, 1)
    second_half = lax.dynamic_slice_in_dim(full_basis, K + narrow_pos * half_cols, half_cols, 1)
    local_panel = jnp.concatenate([first_half, second_half], axis=1)
    pair_block = partner(local_panel, "wide", 0)
    joined = jnp.where(
        position % 2 == 0,
        jnp.concatenate([local_panel, pair_block], axis=0),
        jnp.concatenate([pair_block, local_panel], axis=0),
    )
    quad_block = partner(joined, "wide", 1)
    col_panel = jnp.where(
        position // 2 % 2 == 0,
        jnp.concatenate([joined, quad_block], axis=0),
        jnp.concatenate([quad_block, joined], axis=0),
    )
    products = jnp.dot(
        lax.all_gather(moments, "narrow", axis=1, tiled=True),
        col_panel,
        precision=lax.Precision.HIGHEST,
        preferred_element_type=jnp.float32,
    )
    partials = []
    for slot_index in range(2):
        half_panel = products[:, slot_index * half_cols : (slot_index + 1) * half_cols]
        vectors_half = full_basis[:, slot_index * K : (slot_index + 1) * K]
        partials.append(
            lax.dot_general(
                vectors_half,
                half_panel,
                (((0,), (0,)), ((), ())),
                precision=lax.Precision.HIGHEST,
                preferred_element_type=jnp.float32,
            )
        )
    stacked = jnp.stack(partials)
    slot_pick = (position // 2 + swapped) % 2
    row_part = position % 2
    summed = stacked + partner(stacked, "wide", 0)
    summed = summed + partner(summed, "wide", 1)
    chosen = lax.dynamic_index_in_dim(summed, slot_pick, 0, keepdims=False)
    return lax.dynamic_slice_in_dim(chosen, row_part * (K // 2), K // 2, 0)


def solution(mesh):
    placed = (P("wide", "narrow"), P("wide", "narrow"), P())
    return jax.shard_map(
        body, mesh=mesh, in_specs=placed, out_specs=P("wide", "narrow"), check_vma=False
    )
```

profile of v0, /device:TPU:1, one launch (start us, length us, event | category | flops | bytes accessed | tf_op | source)
XLA Modules:
  0.0 240.8 jit_solution(9913397661584596023)
XLA Ops:
  6.5 0.0 all-gather.3.cloned.1.call-start
  6.5 0.7 all-gather.3.cloned.1.call-update
  7.3 0.0 all-gather.5.cloned.1.call-start
  7.3 0.7 all-gather.5.cloned.1.call-update
  8.0 37.8 %all-gather.3.cloned.1.call-done = f32[512,2048]{1,0:T(8,128)} async-done(((f32[512,512]{1,0:T(8,128)}), f32[512,2048]{1,0:T(8,128)}) %all-gather.3.cloned.1.call-update) | async-done | bytes 4194320 | tf_op jit(solution)/shard_map/all_gather | solution.py:24
  45.9 1.3 constant_dynamic-slice_fusion.1
  47.1 0.1 pad_maximum_fusion.1
  47.3 1.3 collective-permute-start
  48.5 23.4 %collective-permute-done = f32[512,512]{1,0:T(8,128)} collective-permute-done((f32[512,512]{1,0:T(8,128)S(1)}, f32[512,512]{1,0:T(8,128)}, u32[]{:S(2)}, u32[]{:S(2)}) %collective-permute-start) | collective-permute-done | bytes 1048608 | tf_op jit(solution)/shard_map/ppermute | solution.py:13
  71.9 1.9 maximum_select_fusion.2
  73.8 1.3 collective-permute-start.1
  75.1 6.8 %all-gather.5.cloned.1.call-done = f32[512,2048]{1,0:T(8,128)} async-done(((f32[512,512]{1,0:T(8,128)}), f32[512,2048]{1,0:T(8,128)}) %all-gather.5.cloned.1.call-update) | async-done | bytes 4194320 | tf_op jit(solution)/shard_map/all_gather | solution.py:41
  81.9 0.0 copy-start
  81.9 38.1 %collective-permute-done.1 = f32[1024,512]{1,0:T(8,128)} collective-permute-done((f32[1024,512]{1,0:T(8,128)S(1)}, f32[1024,512]{1,0:T(8,128)}, u32[]{:S(2)}, u32[]{:S(2)}) %collective-permute-start.1) | collective-permute-done | bytes 2097184 | tf_op jit(solution)/shard_map/ppermute | solution.py:13
  120.1 17.2 %fusion.17 = f32[512,512]{0,1:T(8,128)S(1)} fusion(f32[512,2048]{1,0:T(8,128)} %all-gather.5.cloned.1.call-done, f32[1024,512]{1,0:T(8,128)} %collective-permute-done.1, f32[1024,512]{1,0:T(8,128)S(1)} %maximum_select_fusion.2, pred[]{:T(512)S(6)} %eq.12), kind=kOutput, calls=%fused_computation.16 | convolution fusion | flops 6445596672 | bytes 9437185 | tf_op jit(solution)/shard_map/dot_general | solution.py:40
  137.3 0.0 copy-done
  137.3 1.9 fusion.14
  139.2 1.9 fusion.11
  141.1 0.2 pad_maximum_fusion
  141.3 0.0 copy-start.1
  141.3 1.3 collective-permute-start.2
  142.6 44.0 %collective-permute-done.2 = f32[2,1024,256]{1,2,0:T(8,128)S(1)} collective-permute-done((f32[2,1024,256]{1,2,0:T(8,128)S(1)}, f32[2,1024,256]{1,2,0:T(8,128)S(1)}, u32[]{:S(2)}, u32[]{:S(2)}) %collective-permute-start.2) | collective-permute-done | bytes 2097184 | tf_op jit(solution)/shard_map/ppermute | solution.py:13
  186.6 0.4 fusion.21
  187.0 1.3 collective-permute-start.3
  188.3 0.0 copy-done.1
  188.3 0.6 dynamic_slice.19
  189.5 42.0 %collective-permute-done.3 = f32[2,1024,256]{1,2,0:T(8,128)} collective-permute-done((f32[2,1024,256]{1,2,0:T(8,128)S(1)}, f32[2,1024,256]{1,2,0:T(8,128)}, u32[]{:S(2)}, u32[]{:S(2)}) %collective-permute-start.3) | collective-permute-done | bytes 2097184 | tf_op jit(solution)/shard_map/ppermute | solution.py:13
  231.5 1.4 dynamic-slice_add_fusion
  233.0 1.0 copy.4
Async XLA Ops:
  6.5 39.3 %all-gather.3.cloned.1.call-start = ((), (), s32[]{:S(2)}) async-start(), calls=%async_computation | async-start | bytes 5242880 | tf_op jit(solution)/shard_map/all_gather | solution.py:24
  7.3 74.6 %all-gather.5.cloned.1.call-start = ((), (), s32[]{:S(2)}) async-start(), calls=%async_computation.1 | async-start | bytes 5242880 | tf_op jit(solution)/shard_map/all_gather | solution.py:41
  47.3 24.6 %collective-permute-start = (f32[512,512]{1,0:T(8,128)S(1)}, f32[512,512]{1,0:T(8,128)}, u32[]{:S(2)}, u32[]{:S(2)}) collective-permute-start(f32[512,512]{1,0:T(8,128)S(1)} %pad_maximum_fusion.1), channel_id=1, source_target_pairs={{0,4},{4,0},{8,12},{12,8},{16,20},{20,16},{24,28},{28,24},{1,5},{5... | collective-permute-start | bytes 3145736 | tf_op jit(solution)/shard_map/ppermute | solution.py:13
  73.8 46.2 %collective-permute-start.1 = (f32[1024,512]{1,0:T(8,128)S(1)}, f32[1024,512]{1,0:T(8,128)}, u32[]{:S(2)}, u32[]{:S(2)}) collective-permute-start(f32[1024,512]{1,0:T(8,128)S(1)} %maximum_select_fusion.2), channel_id=1, source_target_pairs={{0,8},{4,12},{8,0},{12,4},{16,24},{20,28},{24,16},{28,20},{1,9},{5... | collective-permute-start | bytes 6291464 | tf_op jit(solution)/shard_map/ppermute | solution.py:13
  81.9 55.3 %copy-start = (f32[512,2048]{1,0:T(8,128)S(1)}, f32[512,2048]{1,0:T(8,128)}, u32[]{:S(2)}) copy-start(f32[512,2048]{1,0:T(8,128)} %all-gather.3.cloned.1.call-done) | copy-start | bytes 12582916
  141.3 47.0 %copy-start.1 = (s32[2]{0:T(128)S(1)}, s32[2]{0:T(128)}, u32[]{:S(2)}) copy-start(s32[2]{0:T(128)} %param.5) | copy-start | bytes 28
  141.3 45.3 %collective-permute-start.2 = (f32[2,1024,256]{1,2,0:T(8,128)S(1)}, f32[2,1024,256]{1,2,0:T(8,128)S(1)}, u32[]{:S(2)}, u32[]{:S(2)}) collective-permute-start(f32[2,1024,256]{1,2,0:T(8,128)S(1)} %pad_maximum_fusion), channel_id=1, source_target_pairs={{0,4},{4,0},{8,12},{12,8},{16,20},{20,16},{24,28},{28,24},{1,5},{5... | collective-permute-start | bytes 6291464 | tf_op jit(solution)/shard_map/ppermute | solution.py:13
  187.0 44.5 %collective-permute-start.3 = (f32[2,1024,256]{1,2,0:T(8,128)S(1)}, f32[2,1024,256]{1,2,0:T(8,128)}, u32[]{:S(2)}, u32[]{:S(2)}) collective-permute-start(f32[2,1024,256]{1,2,0:T(8,128)S(1)} %fusion.21), channel_id=1, source_target_pairs={{0,8},{4,12},{8,0},{12,4},{16,24},{20,28},{24,16},{28,20},{1,9},{5... | collective-permute-start | bytes 6291464 | tf_op jit(solution)/shard_map/ppermute | solution.py:13
Sparse Core Ops, SparseCore 0:
  8.9 36.9 all-gather.2
  47.4 34.4 all-gather.4
where the time goes:
time: 245 us; the launch traced here: 241 us
  waiting for transfers between devices  194 us (79%)
  matrix products  21 us (9%)
  between operations  14.2 us (6%)
  starting transfers between devices  5.09 us (2%)
  other arithmetic  4.12 us (2%)
  local copies, waits for them, and re-layouts  2.86 us (1%)
    ppermute x4, waiting for transfers between devices, partner(): return lax.ppermute(value, axis, pairs)  147 us
    all_gather x1, waiting for transfers between devices, body(): full_basis = lax.all_gather(eigen_basis, 'narrow', axis=1, tiled=True)  37.8 us
    dot_general x1, matrix products, body(): jnp.dot(lax.all_gather(moments, 'narrow', axis=1, tiled=True), col_panel,...  17.2 us
    all_gather x1, waiting for transfers between devices, body(): lax.all_gather(moments, 'narrow', axis=1, tiled=True)  6.81 us
    ppermute x4, starting transfers between devices, partner(): return lax.ppermute(value, axis, pairs)  5.05 us
  transfers between devices with their start and end apart: 6, of which 6 were waited for; matrix products, arithmetic and copies ran while one was open for 2% of the time, Pallas kernels for 0%

commit v1 on v0

--- a/solution.py
+++ b/solution.py
@@ -1,10 +1,240 @@
 import jax
 import jax.numpy as jnp
 from jax import lax
+from jax.experimental import pallas as pl
+from jax.experimental.pallas import tpu as pltpu
 from jax.sharding import PartitionSpec as P
 
 GROUP_WIDE = 4
 K = 1024
+MESH = pl.DeviceIdType.MESH
+CHUNKS = 4
+
+
+def split(value):
+    high = value.astype(jnp.bfloat16)
+    low = (value - high.astype(jnp.float32)).astype(jnp.bfloat16)
+    return high, low
+
+
+def dot3(left, right):
+    def dot(a, b):
+        return jnp.dot(a, b, preferred_element_type=jnp.float32)
+
+    return dot(left[0], right[0]) + (dot(left[0], right[1]) + dot(left[1], right[0]))
+
+
+def kernel(
+    slot_ref, a_ref, v_ref, o_ref,
+    abuf, vbuf, left, left_t, acc, csend, cmine, crecv, sums, gsame, gother, zsend, zrecv,
+    local_sem, send_sem, recv_sem, extra_sem,
+):
+    rows, cols = a_ref.shape
+    half = rows // 2
+    chunk = csend.shape[1]
+    w = lax.axis_index("wide")
+    n = lax.axis_index("narrow")
+    x = w % 2
+    z = (w // 2) % 2
+    y = n // 2
+    core = n % 2
+    p = w % 4
+    wx = w + 1 - 2 * x
+    wz = w + 2 - 4 * z
+    px = p + 1 - 2 * x
+    pz = p + 2 - 4 * z
+    pd = 3 - p
+    ns = n + 1 - 2 * core
+    ny = n + 2 - 4 * y
+    nd = 3 - n
+    q = 2 * y + core
+
+    barrier = pltpu.get_barrier_semaphore()
+    for target in ((wx, n), (wz, n), (w, ns), (w, ny), (w, nd)):
+        pl.semaphore_signal(barrier, inc=1, device_id=target, device_id_type=MESH)
+
+    local = [
+        pltpu.make_async_copy(v_ref, vbuf.at[p], local_sem.at[0]),
+        pltpu.make_async_copy(v_ref, left.at[core], local_sem.at[1]),
+        pltpu.make_async_copy(a_ref, abuf.at[q], local_sem.at[2]),
+    ]
+    for copy in local:
+        copy.start()
+
+    used = []
+
+    def remote(src, dst, target):
+        index = len(used)
+        used.append(index)
+        return pltpu.make_async_remote_copy(
+            src_ref=src, dst_ref=dst, send_sem=send_sem.at[index], recv_sem=recv_sem.at[index],
+            device_id=target, device_id_type=MESH,
+        )
+
+    top, bottom = pl.ds(0, half), pl.ds(half, half)
+    vx = [remote(v_ref.at[part], vbuf.at[p, part], (wx, n)) for part in (top, bottom)]
+    vz = [remote(v_ref.at[part], vbuf.at[p, part], (wz, n)) for part in (bottom, top)]
+    ay = [remote(a_ref.at[part], abuf.at[q, part], (w, ny)) for part in (top, bottom)]
+    vs = remote(v_ref, left.at[core], (w, ns))
+    as_ = remote(a_ref, abuf.at[q], (w, ns))
+    qy = 2 * (1 - y) + core
+    vxr = remote(vbuf.at[px, top], vbuf.at[px, top], (wz, n))
+    vzr = remote(vbuf.at[pz, bottom], vbuf.at[pz, bottom], (wx, n))
+    ayr = [remote(abuf.at[qy, part], abuf.at[qy, part], (w, ns)) for part in (top, bottom)]
+
+    pl.semaphore_wait(barrier, 5)
+    for copy in (vx[0], vz[0], ay[0], vx[1], vz[1], ay[1], vs, as_):
+        copy.start()
+    for copy in local:
+        copy.wait()
+    left_t[core, 0], left_t[core, 1] = split(left[core].T)
+    vx[0].wait_recv()
+    vxr.start()
+    vz[0].wait_recv()
+    vzr.start()
+    ay[0].wait_recv()
+    ayr[0].start()
+    vs.wait_recv()
+    left_t[1 - core, 0], left_t[1 - core, 1] = split(left[1 - core].T)
+    ay[1].wait_recv()
+    ayr[1].start()
+    as_.wait_recv()
+    ayr[0].wait_recv()
+    ayr[1].wait_recv()
+    acc[...] = dot3(split(abuf[p]), split(vbuf[p]))
+    vx[1].wait_recv()
+    acc[...] += dot3(split(abuf[px]), split(vbuf[px]))
+    vz[1].wait_recv()
+    acc[...] += dot3(split(abuf[pz]), split(vbuf[pz]))
+    vxr.wait_recv()
+    vzr.wait_recv()
+    acc[...] += dot3(split(abuf[pd]), split(vbuf[pd]))
+
+    image = split(acc[...])
+    cx = [remote(csend.at[j], crecv.at[j], (wx, n)) for j in range(CHUNKS)]
+    for j in range(0, CHUNKS, 2):
+        part = pl.ds(j * chunk, 2 * chunk)
+        block = dot3((left_t[1 - x, 0, part], left_t[1 - x, 1, part]), image)
+        csend[j] = block[:chunk]
+        csend[j + 1] = block[chunk:]
+        cx[j].start()
+        cx[j + 1].start()
+    for j in range(0, CHUNKS, 2):
+        part = pl.ds(j * chunk, 2 * chunk)
+        block = dot3((left_t[x, 0, part], left_t[x, 1, part]), image)
+        cmine[j] = block[:chunk]
+        cmine[j + 1] = block[chunk:]
+
+    stays = core == y
+    leaves = core != y
+    keep = [remote(sums.at[j, 1 - core], gsame.at[j], (w, ns)) for j in range(CHUNKS)]
+    cross = [remote(sums.at[j, core], gother.at[j], (w, ny)) for j in range(CHUNKS)]
+    first = len(used) - CHUNKS
+    cross_d = [
+        pltpu.make_async_remote_copy(
+            src_ref=sums.at[j, 1 - core], dst_ref=gother.at[j],
+            send_sem=extra_sem.at[j], recv_sem=recv_sem.at[first + j],
+            device_id=(w, nd), device_id_type=MESH,
+        )
+        for j in range(CHUNKS)
+    ]
+    zc = [remote(zsend.at[j], zrecv.at[j], (wz, n)) for j in range(CHUNKS)]
+
+    swapped = slot_ref[w // GROUP_WIDE]
+    wide_half = gsame.shape[2]
+    same_flag = ((z + swapped + y) % 2) == 0
+
+    def reduce_x(j):
+        cx[j].wait_recv()
+        for k in range(2):
+            piece = pl.ds(k * wide_half, wide_half)
+            sums[j, k] = cmine[j, :, piece] + crecv[j, :, piece]
+
+        @pl.when(stays)
+        def _():
+            keep[j].start()
+            gsame[j] = sums[j, core]
+
+        @pl.when(leaves)
+        def _():
+            cross[j].start()
+            cross_d[j].start()
+
+    def select_z(j):
+        @pl.when(leaves)
+        def _():
+            keep[j].wait_recv()
+
+        cross[j].wait_recv()
+        same, other = gsame[j], gother[j]
+        mask = jnp.full(same.shape, same_flag.astype(jnp.int32)) == 1
+        zsend[j] = jnp.where(mask, other, same)
+        zc[j].start()
+        o_ref[pl.ds(j * chunk, chunk), :] = jnp.where(mask, same, other)
+
+    def finish(j):
+        zc[j].wait_recv()
+        o_ref[pl.ds(j * chunk, chunk), :] += zrecv[j]
+
+    for step in range(CHUNKS + 2):
+        if step < CHUNKS:
+            reduce_x(step)
+        if 0 <= step - 1 < CHUNKS:
+            select_z(step - 1)
+        if 0 <= step - 2 < CHUNKS:
+            finish(step - 2)
+
+    for copy in (*vx, *vz, *ay, vs, as_, vxr, vzr, *ayr, *cx, *zc):
+        copy.wait_send()
+
+    @pl.when(stays)
+    def _():
+        for copy in keep:
+            copy.wait_send()
+
+    @pl.when(leaves)
+    def _():
+        for copy in (*cross, *cross_d):
+            copy.wait_send()
+
+
+def fast_body(moments, eigen_basis, slot_order):
+    rows, cols = moments.shape
+    f32 = jnp.float32
+    chunk = rows // CHUNKS
+    return pl.pallas_call(
+        kernel,
+        out_shape=jax.ShapeDtypeStruct((rows, cols // 2), f32),
+        in_specs=[
+            pl.BlockSpec(memory_space=pltpu.SMEM),
+            pl.BlockSpec(memory_space=pl.ANY),
+            pl.BlockSpec(memory_space=pl.ANY),
+        ],
+        out_specs=pl.BlockSpec(memory_space=pltpu.VMEM),
+        scratch_shapes=[
+            pltpu.VMEM((4, rows, cols), f32),
+            pltpu.VMEM((4, rows, cols), f32),
+            pltpu.VMEM((2, rows, cols), f32),
+            pltpu.VMEM((2, 2, cols, rows), jnp.bfloat16),
+            pltpu.VMEM((rows, cols), f32),
+            pltpu.VMEM((CHUNKS, chunk, cols), f32),
+            pltpu.VMEM((CHUNKS, chunk, cols), f32),
+            pltpu.VMEM((CHUNKS, chunk, cols), f32),
+            pltpu.VMEM((CHUNKS, 2, chunk, cols // 2), f32),
+            pltpu.VMEM((CHUNKS, chunk, cols // 2), f32),
+            pltpu.VMEM((CHUNKS, chunk, cols // 2), f32),
+            pltpu.VMEM((CHUNKS, chunk, cols // 2), f32),
+            pltpu.VMEM((CHUNKS, chunk, cols // 2), f32),
+            pltpu.SemaphoreType.DMA((3,)),
+            pltpu.SemaphoreType.DMA((40,)),
+            pltpu.SemaphoreType.DMA((40,)),
+            pltpu.SemaphoreType.DMA((CHUNKS,)),
+        ],
+        compiler_params=pltpu.CompilerParams(
+            collective_id=0, has_side_effects=True, vmem_limit_bytes=56 * 1024 * 1024
+        ),
+        name="rayleigh",
+    )(slot_order, moments, eigen_basis)
 
 
 def partner(value, axis, stride):
@@ -67,6 +297,7 @@
 
 def solution(mesh):
     placed = (P("wide", "narrow"), P("wide", "narrow"), P())
+    cube = mesh.shape["narrow"] == 4
     return jax.shard_map(
-        body, mesh=mesh, in_specs=placed, out_specs=P("wide", "narrow"), check_vma=False
+        fast_body if cube else body, mesh=mesh, in_specs=placed, out_specs=P("wide", "narrow"), check_vma=False
     )

time: 245 us -> 77.2 us (0.32); the launches traced: 241 us -> 77 us
  waiting for transfers between devices: 194 us -> 0 us
  Pallas kernels: 0 us -> 75.2 us
  matrix products: 21 us -> 0 us
  between operations: 14.2 us -> 0.01 us
  starting transfers between devices: 5.09 us -> 0 us
  other arithmetic: 4.12 us -> 0 us
    ppermute x4 -> x0, waiting for transfers between devices: 147 us -> none  [partner(): return lax.ppermute(value, axis, pairs)]
    pallas_call x0 -> x1, Pallas kernels: none -> 75.2 us  [fast_body(): pl.pallas_call(kernel, out_shape=jax.ShapeDtypeStruct((rows, cols // 2),...]
    all_gather x2 -> x0, waiting for transfers between devices: 44.7 us -> none  [the longest x1 37.8 us: body(): full_basis = lax.all_gather(eigen_basis, 'narrow', axis=1, tiled=True)]
    dot_general x3 -> x0, matrix products: 21 us -> none  [the longest x1 17.2 us: body(): jnp.dot(lax.all_gather(moments, 'narrow', axis=1, tiled=True), col_panel,...]
    ppermute x4 -> x0, starting transfers between devices: 5.05 us -> none  [partner(): return lax.ppermute(value, axis, pairs)]
    dynamic_slice x3 -> x0, local copies, waits for them, and re-layouts: 2.85 us -> none  [the longest x1 1.27 us: body(): lax.dynamic_slice_in_dim(full_basis, narrow_pos * half_cols, half_cols, 1)]
  transfers between devices with their start and end apart: 6 -> 0, of which waited for: 6 -> 0; matrix products, arithmetic and copies ran while one was open for 2% -> 0% of each run, Pallas kernels for 0% -> 0%
where the time goes in v1:
time: 77.2 us; the launch traced here: 77 us
  Pallas kernels  75.2 us (97%)
  local copies, waits for them, and re-layouts  1.87 us (2%)
    pallas_call x1, Pallas kernels, fast_body(): pl.pallas_call(kernel, out_shape=jax.ShapeDtypeStruct((rows, cols // 2),...  75.2 us
    unnamed x1, local copies, waits for them, and re-layouts  1.87 us

profile of v1, /device:TPU:1, one launch (start us, length us, event | category | flops | bytes accessed | tf_op | source)
XLA Modules:
  0.0 77.0 jit_solution(15218002478783981870)
XLA Ops:
  0.0 75.2 %rayleigh.1 = f32[512,256]{1,0:T(8,128)} custom-call(s32[2]{0:T(128)} %slot_ref.1, f32[512,512]{1,0:T(8,128)} %a_ref.1, f32[512,512]{1,0:T(8,128)} %v_ref.1), custom_call_target="tpu_custom_call" | custom-call | tf_op jit(solution)/shard_map/rayleigh/pallas_call | solution.py:205
  75.2 1.9 %copy.5 = f32[512,256]{1,0:T(8,128)} copy(f32[512,256]{1,0:T(8,128)} %rayleigh.1) | data formatting | bytes 1048576

commit v2 on v0

--- a/solution.py
+++ b/solution.py
@@ -1,10 +1,284 @@
 import jax
 import jax.numpy as jnp
 from jax import lax
+from jax.experimental import pallas as pl
+from jax.experimental.pallas import tpu as pltpu
 from jax.sharding import PartitionSpec as P
 
 GROUP_WIDE = 4
 K = 1024
+MESH = pl.DeviceIdType.MESH
+CHUNKS = 4
+PIECES = 4
+RELAYED = 3
+COPIES = 8 * PIECES + 7 * CHUNKS + 2
+
+
+def split(value):
+    high = value.astype(jnp.bfloat16)
+    low = (value - high.astype(jnp.float32)).astype(jnp.bfloat16)
+    return high, low
+
+
+def dot3(left, right):
+    def dot(a, b):
+        return jnp.dot(a, b, preferred_element_type=jnp.float32)
+
+    return dot(left[0], right[0]) + (dot(left[0], right[1]) + dot(left[1], right[0]))
+
+
+def kernel(
+    slot_ref, a_ref, v_ref, o_ref,
+    abuf, aparts, vbuf, left, left_t, csend, cmine, crecv, sums, gsame, gother, zsend, zrecv,
+    local_sem, send_sem, recv_sem,
+):
+    rows, cols = a_ref.shape
+    wide_half = cols // 2
+    piece = rows // PIECES
+    chunk = rows // CHUNKS
+    w = lax.axis_index("wide")
+    n = lax.axis_index("narrow")
+    x = w % 2
+    z = (w // 2) % 2
+    y = n // 2
+    core = n % 2
+    p = w % 4
+    wx = w + 1 - 2 * x
+    wz = w + 2 - 4 * z
+    px = p + 1 - 2 * x
+    pz = p + 2 - 4 * z
+    pd = 3 - p
+    ns = n + 1 - 2 * core
+    ny = n + 2 - 4 * y
+    nd = 3 - n
+    q = 2 * y + core
+    qs = 2 * y + 1 - core
+    qy = 2 * (1 - y) + core
+    qd = 3 - q
+
+    barrier = pltpu.get_barrier_semaphore()
+    for target in ((wx, n), (wz, n), (w, ns), (w, ny), (w, nd)):
+        pl.semaphore_signal(barrier, inc=1, device_id=target, device_id_type=MESH)
+
+    def part(i):
+        return pl.ds(i * piece, piece)
+
+    def side(t):
+        return pl.ds(t * wide_half, wide_half)
+
+    local = [
+        pltpu.make_async_copy(v_ref, left.at[core], local_sem.at[0]),
+        pltpu.make_async_copy(a_ref, abuf.at[q], local_sem.at[1]),
+        pltpu.make_async_copy(v_ref.at[:, side(0)], vbuf.at[p, 0], local_sem.at[2]),
+        pltpu.make_async_copy(v_ref.at[:, side(1)], vbuf.at[p, 1], local_sem.at[3]),
+    ]
+    for copy in local:
+        copy.start()
+
+    used = []
+
+    def remote(src, dst, target):
+        index = len(used)
+        used.append(index)
+        return pltpu.make_async_remote_copy(
+            src_ref=src, dst_ref=dst, send_sem=send_sem.at[index], recv_sem=recv_sem.at[index],
+            device_id=target, device_id_type=MESH,
+        )
+
+    def own(t, i, target):
+        return remote(v_ref.at[part(i), side(t)], vbuf.at[p, t, part(i)], target)
+
+    def relay(t, i, block, target):
+        return remote(vbuf.at[block, t, part(i)], vbuf.at[block, t, part(i)], target)
+
+    vx = [[own(t, i, (wx, n)) for i in range(PIECES)] for t in range(2)]
+    vz = [[own(t, i, (wz, n)) for i in range(PIECES)] for t in range(2)]
+    vxr = [[relay(t, i, px, (wz, n)) for i in range(RELAYED)] for t in range(2)]
+    vzr = [[relay(t, i, pz, (wx, n)) for i in range(RELAYED, PIECES)] for t in range(2)]
+    ay = [remote(a_ref.at[part(i)], abuf.at[q, part(i)], (w, ny)) for i in range(PIECES)]
+    ayr = [remote(abuf.at[qy, part(i)], abuf.at[qy, part(i)], (w, ns)) for i in range(PIECES)]
+    vs = remote(v_ref, left.at[core], (w, ns))
+    as_ = remote(a_ref, abuf.at[q], (w, ns))
+    cx = [[remote(csend.at[t, j], crecv.at[t, j], (wx, n)) for j in range(CHUNKS)] for t in range(2)]
+    keep = [[remote(sums.at[t, j], gsame.at[j], (w, ns)) for j in range(CHUNKS)] for t in range(2)]
+    cross = [[remote(sums.at[t, j], gother.at[j], (w, 2 * (1 - y) + t)) for j in range(CHUNKS)] for t in range(2)]
+    zc = [remote(zsend.at[j], zrecv.at[j], (wz, n)) for j in range(CHUNKS)]
+
+    def start_own(t):
+        for i in range(PIECES):
+            vx[t][i].start()
+            vz[t][PIECES - 1 - i].start()
+
+    def start_relays(t):
+        late = list(range(RELAYED, PIECES))[::-1]
+        for i in range(max(RELAYED, PIECES - RELAYED)):
+            if i < RELAYED:
+                vx[t][i].wait_recv()
+                vxr[t][i].start()
+            if i < PIECES - RELAYED:
+                vz[t][late[i]].wait_recv()
+                vzr[t][late[i] - RELAYED].start()
+
+    pl.semaphore_wait(barrier, 5)
+    start_own(0)
+    for copy in (*ay, vs, as_):
+        copy.start()
+    for copy in local:
+        copy.wait()
+    start_relays(0)
+    start_own(1)
+    ay[0].wait_recv()
+    ayr[0].start()
+    aparts[q, 0], aparts[q, 1] = split(abuf[q])
+    left_t[core, 0], left_t[core, 1] = split(left[core].T)
+    ay[1].wait_recv()
+    ayr[1].start()
+    vs.wait_recv()
+    left_t[1 - core, 0], left_t[1 - core, 1] = split(left[1 - core].T)
+    as_.wait_recv()
+    aparts[qs, 0], aparts[qs, 1] = split(abuf[qs])
+    ay[2].wait_recv()
+    ayr[2].start()
+    ay[3].wait_recv()
+    ayr[3].start()
+    aparts[qy, 0], aparts[qy, 1] = split(abuf[qy])
+    start_relays(1)
+    for copy in ayr:
+        copy.wait_recv()
+    aparts[qd, 0], aparts[qd, 1] = split(abuf[qd])
+
+    def term(t, block):
+        return dot3((aparts[block, 0], aparts[block, 1]), split(vbuf[block, t]))
+
+    def image_of(t):
+        total = term(t, p)
+        for i in range(RELAYED, PIECES):
+            vx[t][i].wait_recv()
+        total += term(t, px)
+        for i in range(RELAYED):
+            vz[t][i].wait_recv()
+        total += term(t, pz)
+        for copy in (*vxr[t], *vzr[t]):
+            copy.wait_recv()
+        return split(total + term(t, pd))
+
+    def send_partials(t, image):
+        for j in range(0, CHUNKS, 2):
+            span = pl.ds(j * chunk, 2 * chunk)
+            block = dot3((left_t[1 - x, 0, span], left_t[1 - x, 1, span]), image)
+            for k in range(2):
+                csend[t, j + k] = block[k * chunk : (k + 1) * chunk]
+                cx[t][j + k].start()
+
+    def keep_partials(t, image):
+        block = dot3((left_t[x, 0], left_t[x, 1]), image)
+        for j in range(CHUNKS):
+            cmine[t, j] = block[j * chunk : (j + 1) * chunk]
+
+    swapped = slot_ref[w // GROUP_WIDE]
+    same_flag = (((z + swapped + y) % 2) == 0).astype(jnp.int32)
+    stays = core == y
+    leaves = core != y
+
+    def reduce_x(t, j):
+        cx[t][j].wait_recv()
+        total = cmine[t, j] + crecv[t, j]
+        sums[t, j] = total
+
+        @pl.when(leaves)
+        def _():
+            cross[t][j].start()
+
+        @pl.when(stays & (core != t))
+        def _():
+            keep[t][j].start()
+
+        @pl.when(stays & (core == t))
+        def _():
+            gsame[j] = total
+
+    def select_z(t, j):
+        @pl.when(core == t)
+        def _():
+            @pl.when(leaves)
+            def _():
+                keep[t][j].wait_recv()
+
+            cross[t][j].wait_recv()
+            same, other = gsame[j], gother[j]
+            mask = jnp.full(same.shape, same_flag) == 1
+            zsend[j] = jnp.where(mask, other, same)
+            zc[j].start()
+            o_ref[pl.ds(j * chunk, chunk), :] = jnp.where(mask, same, other)
+
+    def finish(t, j):
+        @pl.when(core == t)
+        def _():
+            zc[j].wait_recv()
+            o_ref[pl.ds(j * chunk, chunk), :] += zrecv[j]
+
+    image = image_of(0)
+    send_partials(0, image)
+    keep_partials(0, image)
+    image = image_of(1)
+    send_partials(1, image)
+    keep_partials(1, image)
+
+    steps = [(t, j) for t in range(2) for j in range(CHUNKS)]
+    for step in range(len(steps) + 2):
+        if step < len(steps):
+            reduce_x(*steps[step])
+        if 0 <= step - 1 < len(steps):
+            select_z(*steps[step - 1])
+        if 0 <= step - 2 < len(steps):
+            finish(*steps[step - 2])
+
+    flat = [copy for group in (*vx, *vz, *vxr, *vzr, *cx) for copy in group]
+    for copy in (*flat, *ay, *ayr, vs, as_, *zc):
+        copy.wait_send()
+    for t in range(2):
+        @pl.when(leaves)
+        def _():
+            for copy in cross[t]:
+                copy.wait_send()
+
+        @pl.when(stays & (core != t))
+        def _():
+            for copy in keep[t]:
+                copy.wait_send()
+
+
+def fast_body(moments, eigen_basis, slot_order):
+    rows, cols = moments.shape
+    f32 = jnp.float32
+    chunk = rows // CHUNKS
+    wide_half = cols // 2
+    return pl.pallas_call(
+        kernel,
+        out_shape=jax.ShapeDtypeStruct((rows, wide_half), f32),
+        in_specs=[
+            pl.BlockSpec(memory_space=pltpu.SMEM),
+            pl.BlockSpec(memory_space=pl.ANY),
+            pl.BlockSpec(memory_space=pl.ANY),
+        ],
+        out_specs=pl.BlockSpec(memory_space=pltpu.VMEM),
+        scratch_shapes=[
+            pltpu.VMEM((4, rows, cols), f32),
+            pltpu.VMEM((4, 2, rows, cols), jnp.bfloat16),
+            pltpu.VMEM((4, 2, rows, wide_half), f32),
+            pltpu.VMEM((2, rows, cols), f32),
+            pltpu.VMEM((2, 2, cols, rows), jnp.bfloat16),
+            *[pltpu.VMEM((2, CHUNKS, chunk, wide_half), f32)] * 4,
+            *[pltpu.VMEM((CHUNKS, chunk, wide_half), f32)] * 4,
+            pltpu.SemaphoreType.DMA((4,)),
+            pltpu.SemaphoreType.DMA((COPIES,)),
+            pltpu.SemaphoreType.DMA((COPIES,)),
+        ],
+        compiler_params=pltpu.CompilerParams(
+            collective_id=0, has_side_effects=True, vmem_limit_bytes=56 * 1024 * 1024
+        ),
+        name="rayleigh",
+    )(slot_order, moments, eigen_basis)
 
 
 def partner(value, axis, stride):
@@ -67,6 +341,7 @@
 
 def solution(mesh):
     placed = (P("wide", "narrow"), P("wide", "narrow"), P())
+    cube = mesh.shape["narrow"] == 4
     return jax.shard_map(
-        body, mesh=mesh, in_specs=placed, out_specs=P("wide", "narrow"), check_vma=False
+        fast_body if cube else body, mesh=mesh, in_specs=placed, out_specs=P("wide", "narrow"), check_vma=False
     )

time: 245 us -> 74.2 us (0.30); the launches traced: 241 us -> 74 us
  waiting for transfers between devices: 194 us -> 0 us
  Pallas kernels: 0 us -> 72.1 us
  matrix products: 21 us -> 0 us
  between operations: 14.2 us -> 0.01 us
  starting transfers between devices: 5.09 us -> 0 us
  other arithmetic: 4.12 us -> 0 us
    ppermute x4 -> x0, waiting for transfers between devices: 147 us -> none  [partner(): return lax.ppermute(value, axis, pairs)]
    pallas_call x0 -> x1, Pallas kernels: none -> 72.1 us  [fast_body(): pl.pallas_call(kernel, out_shape=jax.ShapeDtypeStruct((rows, wide_half),...]
    all_gather x2 -> x0, waiting for transfers between devices: 44.7 us -> none  [the longest x1 37.8 us: body(): full_basis = lax.all_gather(eigen_basis, 'narrow', axis=1, tiled=True)]
    dot_general x3 -> x0, matrix products: 21 us -> none  [the longest x1 17.2 us: body(): jnp.dot(lax.all_gather(moments, 'narrow', axis=1, tiled=True), col_panel,...]
    ppermute x4 -> x0, starting transfers between devices: 5.05 us -> none  [partner(): return lax.ppermute(value, axis, pairs)]
    dynamic_slice x3 -> x0, local copies, waits for them, and re-layouts: 2.85 us -> none  [the longest x1 1.27 us: body(): lax.dynamic_slice_in_dim(full_basis, narrow_pos * half_cols, half_cols, 1)]
  transfers between devices with their start and end apart: 6 -> 0, of which waited for: 6 -> 0; matrix products, arithmetic and copies ran while one was open for 2% -> 0% of each run, Pallas kernels for 0% -> 0%
where the time goes in v2:
time: 74.2 us; the launch traced here: 74 us
  Pallas kernels  72.1 us (97%)
  local copies, waits for them, and re-layouts  1.87 us (3%)
    pallas_call x1, Pallas kernels, fast_body(): pl.pallas_call(kernel, out_shape=jax.ShapeDtypeStruct((rows, wide_half),...  72.1 us
    unnamed x1, local copies, waits for them, and re-layouts  1.87 us

profile of v2, /device:TPU:1, one launch (start us, length us, event | category | flops | bytes accessed | tf_op | source)
XLA Modules:
  0.0 74.0 jit_solution(2071523522128930819)
XLA Ops:
  0.0 72.1 %rayleigh.1 = f32[512,256]{1,0:T(8,128)} custom-call(s32[2]{0:T(128)} %slot_ref.1, f32[512,512]{1,0:T(8,128)} %a_ref.1, f32[512,512]{1,0:T(8,128)} %v_ref.1), custom_call_target="tpu_custom_call" | custom-call | tf_op jit(solution)/shard_map/rayleigh/pallas_call | solution.py:256
  72.1 1.9 %copy.5 = f32[512,256]{1,0:T(8,128)} copy(f32[512,256]{1,0:T(8,128)} %rayleigh.1) | data formatting | bytes 1048576

commit v3 on v2

--- a/solution.py
+++ b/solution.py
@@ -8,10 +8,12 @@
 GROUP_WIDE = 4
 K = 1024
 MESH = pl.DeviceIdType.MESH
-CHUNKS = 4
-PIECES = 4
-RELAYED = 3
-COPIES = 8 * PIECES + 7 * CHUNKS + 2
+CHUNKS = 8
+PIECES = 8
+RELAYED = 5
+LAG = 2
+A_PIECES = 4
+COPIES = 6 * PIECES + 2 * A_PIECES + 7 * CHUNKS + 2
 
 
 def split(value):
@@ -95,8 +97,9 @@
     vz = [[own(t, i, (wz, n)) for i in range(PIECES)] for t in range(2)]
     vxr = [[relay(t, i, px, (wz, n)) for i in range(RELAYED)] for t in range(2)]
     vzr = [[relay(t, i, pz, (wx, n)) for i in range(RELAYED, PIECES)] for t in range(2)]
-    ay = [remote(a_ref.at[part(i)], abuf.at[q, part(i)], (w, ny)) for i in range(PIECES)]
-    ayr = [remote(abuf.at[qy, part(i)], abuf.at[qy, part(i)], (w, ns)) for i in range(PIECES)]
+    a_rows = [pl.ds(i * (rows // A_PIECES), rows // A_PIECES) for i in range(A_PIECES)]
+    ay = [remote(a_ref.at[span], abuf.at[q, span], (w, ny)) for span in a_rows]
+    ayr = [remote(abuf.at[qy, span], abuf.at[qy, span], (w, ns)) for span in a_rows]
     vs = remote(v_ref, left.at[core], (w, ns))
     as_ = remote(a_ref, abuf.at[q], (w, ns))
     cx = [[remote(csend.at[t, j], crecv.at[t, j], (wx, n)) for j in range(CHUNKS)] for t in range(2)]
@@ -163,10 +166,11 @@
         return split(total + term(t, pd))
 
     def send_partials(t, image):
-        for j in range(0, CHUNKS, 2):
-            span = pl.ds(j * chunk, 2 * chunk)
+        group = CHUNKS // 2
+        for j in range(0, CHUNKS, group):
+            span = pl.ds(j * chunk, group * chunk)
             block = dot3((left_t[1 - x, 0, span], left_t[1 - x, 1, span]), image)
-            for k in range(2):
+            for k in range(group):
                 csend[t, j + k] = block[k * chunk : (k + 1) * chunk]
                 cx[t][j + k].start()
 
@@ -224,14 +228,18 @@
     send_partials(1, image)
     keep_partials(1, image)
 
-    steps = [(t, j) for t in range(2) for j in range(CHUNKS)]
-    for step in range(len(steps) + 2):
-        if step < len(steps):
-            reduce_x(*steps[step])
-        if 0 <= step - 1 < len(steps):
-            select_z(*steps[step - 1])
-        if 0 <= step - 2 < len(steps):
-            finish(*steps[step - 2])
+    for j in range(CHUNKS):
+        reduce_x(0, j)
+    for j in range(CHUNKS):
+        select_z(0, j)
+    for j in range(CHUNKS + LAG):
+        if j < CHUNKS:
+            reduce_x(1, j)
+        if j >= LAG:
+            select_z(1, j - LAG)
+    for t in range(2):
+        for j in range(CHUNKS):
+            finish(t, j)
 
     flat = [copy for group in (*vx, *vz, *vxr, *vzr, *cx) for copy in group]
     for copy in (*flat, *ay, *ayr, vs, as_, *zc):

time: 74.2 us -> 69.9 us (0.942)
  Pallas kernels: 72.1 us -> 67.8 us
    pallas_call x1, Pallas kernels: 72.1 us -> 67.8 us  [fast_body(): pl.pallas_call(kernel, out_shape=jax.ShapeDtypeStruct((rows, wide_half),...]
where the time goes in v3:
time: 69.9 us; the launch traced here: 69.7 us
  Pallas kernels  67.8 us (97%)
  local copies, waits for them, and re-layouts  1.87 us (3%)
    pallas_call x1, Pallas kernels, fast_body(): pl.pallas_call(kernel, out_shape=jax.ShapeDtypeStruct((rows, wide_half),...  67.8 us
    unnamed x1, local copies, waits for them, and re-layouts  1.87 us

profile of v3, /device:TPU:1, one launch (start us, length us, event | category | flops | bytes accessed | tf_op | source)
XLA Modules:
  0.0 69.7 jit_solution(7718875294020719190)
XLA Ops:
  0.0 67.8 %rayleigh.1 = f32[512,256]{1,0:T(8,128)} custom-call(s32[2]{0:T(128)} %slot_ref.1, f32[512,512]{1,0:T(8,128)} %a_ref.1, f32[512,512]{1,0:T(8,128)} %v_ref.1), custom_call_target="tpu_custom_call" | custom-call | tf_op jit(solution)/shard_map/rayleigh/pallas_call | solution.py:264
  67.8 1.9 %copy.5 = f32[512,256]{1,0:T(8,128)} copy(f32[512,256]{1,0:T(8,128)} %rayleigh.1) | data formatting | bytes 1048576

commit v4 on v3

--- a/solution.py
+++ b/solution.py
@@ -11,9 +11,11 @@
 CHUNKS = 8
 PIECES = 8
 RELAYED = 5
-LAG = 2
+LAG = 1
+SPLIT = 3
+DIRECT = CHUNKS - SPLIT
 A_PIECES = 4
-COPIES = 6 * PIECES + 2 * A_PIECES + 7 * CHUNKS + 2
+COPIES = 6 * PIECES + 2 * A_PIECES + 7 * CHUNKS + 2 + 3 * SPLIT
 
 
 def split(value):
@@ -32,12 +34,14 @@
 def kernel(
     slot_ref, a_ref, v_ref, o_ref,
     abuf, aparts, vbuf, left, left_t, csend, cmine, crecv, sums, gsame, gother, zsend, zrecv,
+    fpart, frecv, fsend, fback, fsums, fsame, fother, fzsend, fzrecv,
     local_sem, send_sem, recv_sem,
 ):
     rows, cols = a_ref.shape
     wide_half = cols // 2
     piece = rows // PIECES
     chunk = rows // CHUNKS
+    sub = chunk // 2
     w = lax.axis_index("wide")
     n = lax.axis_index("narrow")
     x = w % 2
@@ -102,10 +106,17 @@
     ayr = [remote(abuf.at[qy, span], abuf.at[qy, span], (w, ns)) for span in a_rows]
     vs = remote(v_ref, left.at[core], (w, ns))
     as_ = remote(a_ref, abuf.at[q], (w, ns))
-    cx = [[remote(csend.at[t, j], crecv.at[t, j], (wx, n)) for j in range(CHUNKS)] for t in range(2)]
-    keep = [[remote(sums.at[t, j], gsame.at[j], (w, ns)) for j in range(CHUNKS)] for t in range(2)]
-    cross = [[remote(sums.at[t, j], gother.at[j], (w, 2 * (1 - y) + t)) for j in range(CHUNKS)] for t in range(2)]
+    cx = [[remote(csend.at[t, j], crecv.at[t, j], (wx, n)) for j in range(count)] for t, count in enumerate((CHUNKS, DIRECT))]
+    keep = [[remote(sums.at[t, j], gsame.at[j], (w, ns)) for j in range(count)] for t, count in enumerate((CHUNKS, DIRECT))]
+    cross = [[remote(sums.at[t, j], gother.at[j], (w, 2 * (1 - y) + t)) for j in range(count)] for t, count in enumerate((CHUNKS, DIRECT))]
     zc = [remote(zsend.at[j], zrecv.at[j], (wz, n)) for j in range(CHUNKS)]
+    mine_rows = pl.ds(pl.multiple_of(z * sub, sub), sub)
+    theirs_rows = pl.ds(pl.multiple_of((1 - z) * sub, sub), sub)
+    zf = [[remote(fpart.at[i, a, theirs_rows], frecv.at[i, a], (wz, n)) for a in range(2)] for i in range(SPLIT)]
+    xf = [remote(fsend.at[i], fback.at[i], (wx, n)) for i in range(SPLIT)]
+    keepf = [remote(fsums.at[i], fsame.at[i], (w, ns)) for i in range(SPLIT)]
+    crossf = [remote(fsums.at[i], fother.at[i], (w, 2 * (1 - y) + 1)) for i in range(SPLIT)]
+    zf2 = [remote(fzsend.at[i], fzrecv.at[i], (wz, n)) for i in range(SPLIT)]
 
     def start_own(t):
         for i in range(PIECES):
@@ -171,13 +182,23 @@
             span = pl.ds(j * chunk, group * chunk)
             block = dot3((left_t[1 - x, 0, span], left_t[1 - x, 1, span]), image)
             for k in range(group):
-                csend[t, j + k] = block[k * chunk : (k + 1) * chunk]
-                cx[t][j + k].start()
+                value = block[k * chunk : (k + 1) * chunk]
+                if j + k < len(cx[t]):
+                    csend[t, j + k] = value
+                    cx[t][j + k].start()
+                else:
+                    fpart[j + k - DIRECT, 0] = value
+                    zf[j + k - DIRECT][0].start()
 
     def keep_partials(t, image):
         block = dot3((left_t[x, 0], left_t[x, 1]), image)
         for j in range(CHUNKS):
-            cmine[t, j] = block[j * chunk : (j + 1) * chunk]
+            value = block[j * chunk : (j + 1) * chunk]
+            if j < len(cx[t]):
+                cmine[t, j] = value
+            else:
+                fpart[j - DIRECT, 1] = value
+                zf[j - DIRECT][1].start()
 
     swapped = slot_ref[w // GROUP_WIDE]
     same_flag = (((z + swapped + y) % 2) == 0).astype(jnp.int32)
@@ -221,6 +242,51 @@
             zc[j].wait_recv()
             o_ref[pl.ds(j * chunk, chunk), :] += zrecv[j]
 
+    def split_x(i):
+        zf[i][0].wait_recv()
+        fsend[i] = fpart[i, 0, mine_rows] + frecv[i, 0]
+        xf[i].start()
+
+    def split_y(i):
+        zf[i][1].wait_recv()
+        xf[i].wait_recv()
+        total = fpart[i, 1, mine_rows] + frecv[i, 1] + fback[i]
+        fsums[i] = total
+
+        @pl.when(leaves)
+        def _():
+            crossf[i].start()
+
+        @pl.when(stays & (core == 0))
+        def _():
+            keepf[i].start()
+
+        @pl.when(stays & (core == 1))
+        def _():
+            fsame[i] = total
+
+    def split_z(i):
+        @pl.when(core == 1)
+        def _():
+            @pl.when(leaves)
+            def _():
+                keepf[i].wait_recv()
+
+            crossf[i].wait_recv()
+            same, other = fsame[i], fother[i]
+            mask = jnp.full(same.shape, same_flag) == 1
+            fzsend[i] = jnp.where(mask, other, same)
+            zf2[i].start()
+            base = (DIRECT + i) * chunk + z * sub
+            o_ref[pl.ds(pl.multiple_of(base, sub), sub), :] = jnp.where(mask, same, other)
+
+    def split_finish(i):
+        @pl.when(core == 1)
+        def _():
+            zf2[i].wait_recv()
+            base = (DIRECT + i) * chunk + (1 - z) * sub
+            o_ref[pl.ds(pl.multiple_of(base, sub), sub), :] = fzrecv[i]
+
     image = image_of(0)
     send_partials(0, image)
     keep_partials(0, image)
@@ -232,18 +298,51 @@
         reduce_x(0, j)
     for j in range(CHUNKS):
         select_z(0, j)
-    for j in range(CHUNKS + LAG):
-        if j < CHUNKS:
-            reduce_x(1, j)
+    for i in range(SPLIT):
+        split_x(i)
+    for j in range(DIRECT):
+        reduce_x(1, j)
         if j >= LAG:
             select_z(1, j - LAG)
-    for t in range(2):
-        for j in range(CHUNKS):
-            finish(t, j)
-
-    flat = [copy for group in (*vx, *vz, *vxr, *vzr, *cx) for copy in group]
-    for copy in (*flat, *ay, *ayr, vs, as_, *zc):
+    for i in range(SPLIT):
+        split_y(i)
+        if i < LAG:
+            select_z(1, DIRECT - LAG + i)
+        else:
+            split_z(i - LAG)
+    for i in range(SPLIT - LAG, SPLIT):
+        split_z(i)
+    for j in range(CHUNKS):
+        finish(0, j)
+    for j in range(DIRECT):
+        finish(1, j)
+    for i in range(SPLIT):
+        split_finish(i)
+
+    flat = [copy for group in (*vx, *vz, *vxr, *vzr, *cx, *zf) for copy in group]
+    for copy in (*flat, *ay, *ayr, vs, as_, *xf, *zc[:DIRECT]):
         copy.wait_send()
+
+    @pl.when(core == 0)
+    def _():
+        for copy in zc[DIRECT:]:
+            copy.wait_send()
+
+    @pl.when(core == 1)
+    def _():
+        for copy in zf2:
+            copy.wait_send()
+
+    @pl.when(leaves)
+    def _():
+        for copy in crossf:
+            copy.wait_send()
+
+    @pl.when(stays & (core == 0))
+    def _():
+        for copy in keepf:
+            copy.wait_send()
+
     for t in range(2):
         @pl.when(leaves)
         def _():
@@ -278,6 +377,9 @@
             pltpu.VMEM((2, 2, cols, rows), jnp.bfloat16),
             *[pltpu.VMEM((2, CHUNKS, chunk, wide_half), f32)] * 4,
             *[pltpu.VMEM((CHUNKS, chunk, wide_half), f32)] * 4,
+            pltpu.VMEM((SPLIT, 2, chunk, wide_half), f32),
+            pltpu.VMEM((SPLIT, 2, chunk // 2, wide_half), f32),
+            *[pltpu.VMEM((SPLIT, chunk // 2, wide_half), f32)] * 7,
             pltpu.SemaphoreType.DMA((4,)),
             pltpu.SemaphoreType.DMA((COPIES,)),
             pltpu.SemaphoreType.DMA((COPIES,)),

time: 69.9 us -> 67.2 us (0.961)
  Pallas kernels: 67.8 us -> 65.2 us
    pallas_call x1, Pallas kernels: 67.8 us -> 65.2 us  [fast_body(): pl.pallas_call(kernel, out_shape=jax.ShapeDtypeStruct((rows, wide_half),...]
where the time goes in v4:
time: 67.2 us; the launch traced here: 67.1 us
  Pallas kernels  65.2 us (97%)
  local copies, waits for them, and re-layouts  1.87 us (3%)
    pallas_call x1, Pallas kernels, fast_body(): pl.pallas_call(kernel, out_shape=jax.ShapeDtypeStruct((rows, wide_half),...  65.2 us
    unnamed x1, local copies, waits for them, and re-layouts  1.87 us

profile of v4, /device:TPU:1, one launch (start us, length us, event | category | flops | bytes accessed | tf_op | source)
XLA Modules:
  0.0 67.1 jit_solution(6058733442470897177)
XLA Ops:
  0.0 65.2 %rayleigh.1 = f32[512,256]{1,0:T(8,128)} custom-call(s32[2]{0:T(128)} %slot_ref.1, f32[512,512]{1,0:T(8,128)} %a_ref.1, f32[512,512]{1,0:T(8,128)} %v_ref.1), custom_call_target="tpu_custom_call" | custom-call | tf_op jit(solution)/shard_map/rayleigh/pallas_call | solution.py:363
  65.2 1.9 %copy.5 = f32[512,256]{1,0:T(8,128)} copy(f32[512,256]{1,0:T(8,128)} %rayleigh.1) | data formatting | bytes 1048576

commit v5 on v4

--- a/solution.py
+++ b/solution.py
@@ -12,7 +12,7 @@
 PIECES = 8
 RELAYED = 5
 LAG = 1
-SPLIT = 3
+SPLIT = 4
 DIRECT = CHUNKS - SPLIT
 A_PIECES = 4
 COPIES = 6 * PIECES + 2 * A_PIECES + 7 * CHUNKS + 2 + 3 * SPLIT

time: 67.2 us -> 66.7 us (level)
  no operation moved by 1% of the time
where the time goes in v5:
time: 66.7 us; the launch traced here: 66.5 us
  Pallas kernels  64.6 us (97%)
  local copies, waits for them, and re-layouts  1.87 us (3%)
    pallas_call x1, Pallas kernels, fast_body(): pl.pallas_call(kernel, out_shape=jax.ShapeDtypeStruct((rows, wide_half),...  64.6 us
    unnamed x1, local copies, waits for them, and re-layouts  1.87 us

profile of v5, /device:TPU:1, one launch (start us, length us, event | category | flops | bytes accessed | tf_op | source)
XLA Modules:
  0.0 66.5 jit_solution(6025409759459402690)
XLA Ops:
  0.0 64.6 %rayleigh.1 = f32[512,256]{1,0:T(8,128)} custom-call(s32[2]{0:T(128)} %slot_ref.1, f32[512,512]{1,0:T(8,128)} %a_ref.1, f32[512,512]{1,0:T(8,128)} %v_ref.1), custom_call_target="tpu_custom_call" | custom-call | tf_op jit(solution)/shard_map/rayleigh/pallas_call | solution.py:363
  64.6 1.9 %copy.5 = f32[512,256]{1,0:T(8,128)} copy(f32[512,256]{1,0:T(8,128)} %rayleigh.1) | data formatting | bytes 1048576
